TPU v7x, 32 devices: a whole 2x2x4 slice. The times are simulated.
32 devices in a mesh: expert: 4 (over y, core), dp: 8 (over z, x).
Axes of the slice: x: 2, y: 2, z: 4, core: 2. Of those that a mesh axis runs over, the one named last changes fastest.
Arguments:
- tokens: bfloat16 [2048, 3584], P(('dp', 'expert')), parts along dimension 0, may hold values from -6 to 6
- expert_ids: int32 [2048, 1], P(('dp', 'expert')), parts along dimension 0, may hold values from 0 to 3; in each aligned block of 64 rows (0 to 63, 64 to 127, ...) at most 18 rows name the same one
- combine: bfloat16 [2048, 1], P(('dp', 'expert')), parts along dimension 0, may hold values from 0.19921875 to 1
- w_gate: bfloat16 [3584, 8192], P(None, 'expert'), may hold values from -0.09375 to 0.09375
- w_up: bfloat16 [3584, 8192], P(None, 'expert'), may hold values from -0.09375 to 0.09375
- w_down: bfloat16 [8192, 3584], P('expert'), may hold values from -0.125 to 0.125
Outputs:
- mixed: bfloat16 [2048, 3584], P(('dp', 'expert')), parts along dimension 0
There are 8 independent parts, one for each index of `dp`. A program takes and returns all parts, laid end to end along the dimension named above; an argument that names none is the same for every part. Nothing has to cross between parts.
Inputs may be any that keep to these rules, and one draw needn't show every extreme that they name: `expert_ids`: each token names one expert. Among the 64 tokens of one device (aligned blocks of rows) no expert is named more than 18 times, a bound that some block reaches.
All inputs are finite; a program needn't handle non-finite values.
Results may differ from a plain program's by a relative error of at most 0.0057.
Values may be sent and summed in bfloat16 or wider, within the bound.
A program may use at most 128 MiB of HBM per device.

v0:
```python
import jax
import jax.numpy as jnp
from jax import lax
from jax.sharding import PartitionSpec as P

EXPERTS = 4
TOP = 1
CAP = 18


def local(tokens, expert_ids, combine, w_gate, w_up, w_down):
    devices = lax.axis_size("expert")
    span_size = devices // EXPERTS
    model_width = tokens.shape[1]
    token_count = tokens.shape[0]
    flat_ids = expert_ids.reshape(-1)
    labels = jnp.arange(EXPERTS, dtype=jnp.int32)
    member = (flat_ids[:, None] == labels[None, :]).astype(jnp.int32)
    rank_table = jnp.cumsum(member, axis=0) - 1
    positions = jnp.sum(member * rank_table, axis=1)
    slot_ids = jnp.arange(CAP, dtype=jnp.int32)
    placed = (member.T[:, None, :] == 1) & (positions[None, None, :] == slot_ids[None, :, None])
    repeated = jnp.repeat(tokens, TOP, axis=0)
    outgoing = jnp.einsum(
        "ecf,fd->ecd", placed.astype(jnp.bfloat16), repeated, preferred_element_type=jnp.float32
    ).astype(jnp.bfloat16)
    outgoing = jnp.repeat(outgoing, span_size, axis=0)
    arrived = lax.all_to_all(outgoing, "expert", split_axis=0, concat_axis=0, tiled=True)
    slot_count = arrived.shape[1]
    row_block = arrived.reshape(-1, model_width)
    gate_values = jnp.dot(row_block, w_gate, preferred_element_type=jnp.float32)
    up_values = jnp.dot(row_block, w_up, preferred_element_type=jnp.float32)
    hidden = (jax.nn.silu(gate_values) * up_values).astype(jnp.bfloat16)
    result = (
        jnp.dot(hidden, w_down, preferred_element_type=jnp.float32)
        .astype(jnp.bfloat16)
        .reshape(devices, slot_count, model_width)
    )
    returned_rows = lax.all_to_all(result, "expert", split_axis=0, concat_axis=0, tiled=True)
    summed = jnp.sum(
        returned_rows.astype(jnp.float32).reshape(EXPERTS, span_size, CAP, model_width), axis=1
    )
    weighted = placed.astype(jnp.float32) * combine.astype(jnp.float32).reshape(-1)[None, None, :]
    entry_rows = jnp.einsum("ecf,ecd->fd", weighted, summed, precision=lax.Precision.HIGHEST)
    mixed_rows = jnp.sum(entry_rows.reshape(token_count, TOP, model_width), axis=1)
    return mixed_rows.astype(jnp.bfloat16)


def solution(mesh):
    placed = (
        P(("dp", "expert"), None),
        P(("dp", "expert"), None),
        P(("dp", "expert"), None),
        P(None, "expert"),
        P(None, "expert"),
        P("expert", None),
    )
    return jax.shard_map(
        local, mesh=mesh, in_specs=placed, out_specs=P(("dp", "expert"), None), check_vma=False
    )
```

profile of v0, /device:TPU:0, one launch (start us, length us, event | category | flops | bytes accessed | tf_op | source)
XLA Modules:
  0.0 56.4 jit_solution(2965514269756863854)
XLA Ops:
  0.0 0.0 copy-start
  0.0 0.8 %fusion.5 = s32[64,4]{1,0:T(8,128)S(1)} fusion(s32[64]{0:T(128)} %bitcast.17), kind=kLoop, calls=%fused_computation.12 | loop fusion | flops 512 | bytes 1280 | tf_op jit(solution)/shard_map/convert_element_type | solution.py:18
  0.8 0.7 %convert_compare_fusion = pred[4,64]{1,0:T(4,128)(4,1)S(1)} fusion(s32[64]{0:T(128)} %bitcast.18), kind=kLoop, calls=%fused_computation.20 | loop fusion | flops 768 | bytes 512 | tf_op jit(solution)/shard_map/eq | solution.py:22
  1.4 0.1 reduce_window_sum.11
  1.5 0.8 %select_reduce_fusion = s32[64]{0:T(128)S(1)} fusion(s32[64,4]{1,0:T(8,128)S(1)} %reduce_window_sum.11, s32[64]{0:T(128)} %bitcast.19), kind=kLoop, calls=%fused_computation.10 | loop fusion | flops 960 | bytes 1536 | tf_op jit(solution)/shard_map/reduce_sum | solution.py:20
  2.4 0.0 copy-done
  2.4 0.3 convolution_convert_fusion
  2.7 14.6 %all_to_all.10 = bf16[4,18,3584]{2,1,0:T(8,128)(2,1)S(1)} all-to-all(bf16[4,18,3584]{2,1,0:T(8,128)(2,1)S(1)} %convolution_convert_fusion), channel_id=1, replica_groups=mesh['expert'=4,'dp'=8] {'expert'}, dimensions={0} | all-to-all | bytes 1032192 | tf_op jit(solution)/shard_map/all_to_all | solution.py:28
  17.4 0.2 reshape.60
  17.5 7.8 %fusion.14 = f32[72,2048]{1,0:T(8,128)S(1)} fusion(bf16[72,3584]{1,0:T(8,128)(2,1)S(1)} %reshape.60, bf16[3584,2048]{1,0:T(8,128)(2,1)} %param.9), kind=kOutput, calls=%fused_computation.25 | convolution fusion | flops 1056964608 | bytes 15785984 | tf_op jit(solution)/shard_map/dot_general | solution.py:31
  25.4 0.0 copy-start.1
  25.4 14.6 %convolution_convert_fusion.1 = bf16[72,3584]{1,0:T(8,128)(2,1)S(1)} fusion(bf16[2048,3584]{1,0:T(8,128)(2,1)} %param.11, bf16[72,3584]{1,0:T(8,128)(2,1)S(1)} %reshape.60, bf16[3584,2048]{1,0:T(8,128)(2,1)} %param.10, f32[72,2048]{1,0:T(8,128)S(1)} %fusion.14), kind=kOutput, calls=%fused_computation.2 | convolution fusion | flops 2115072000 | bytes 30982144 | tf_op jit(solution)/shard_map/dot_general | solution.py:35
  40.0 1.0 %reshape.61 = bf16[4,18,3584]{2,1,0:T(8,128)(2,1)} reshape(bf16[72,3584]{1,0:T(8,128)(2,1)S(1)} %convolution_convert_fusion.1) | data formatting | bytes 1032192 | tf_op jit(solution)/shard_map/reshape | solution.py:37
  41.0 3.5 %all-to-all-start.1 = ((bf16[4,18,3584]{2,1,0:T(8,128)(2,1)}), bf16[4,18,3584]{2,1,0:T(8,128)(2,1)S(1)}, u32[]{:S(2)}, u32[]{:S(2)}) async-start(bf16[4,18,3584]{2,1,0:T(8,128)(2,1)} %reshape.61), calls=%async_computation.1 | async-start | bytes 1376256 | tf_op jit(solution)/shard_map/all_to_all | solution.py:39
  44.5 0.0 copy-done.1
  44.5 10.5 %all-to-all-done.1 = bf16[4,18,3584]{2,1,0:T(8,128)(2,1)S(1)} async-done(((bf16[4,18,3584]{2,1,0:T(8,128)(2,1)}), bf16[4,18,3584]{2,1,0:T(8,128)(2,1)S(1)}, u32[]{:S(2)}, u32[]{:S(2)}) %all-to-all-start.1) | async-done | bytes 516128 | tf_op jit(solution)/shard_map/all_to_all | solution.py:39
  55.0 1.4 %fusion = bf16[64,3584]{1,0:T(8,128)(2,1)} fusion(bf16[4,18,3584]{2,1,0:T(8,128)(2,1)S(1)} %all-to-all-done.1, f32[64]{0:T(128)S(1)} %bitcast_convert_fusion, pred[18,64]{1,0:T(8,128)(4,1)S(1)} %iota_compare_fusion.1, pred[4,64]{1,0:T(4,128)(4,1)S(1)} %convert_compare_fusion), kind=kOutput, calls=%fused_computation.3 | convolution fusion | flops 198419456 | bytes 976512 | tf_op jit(solution)/shard_map/ecf,ecd->fd/dot_general | solution.py:44
  (2 shorter events, 0.0 us)
Async XLA Ops:
  0.0 2.4 %copy-start = (bf16[64,3584]{1,0:T(8,128)(2,1)S(1)}, bf16[64,3584]{1,0:T(8,128)(2,1)}, u32[]{:S(2)}) copy-start(bf16[64,3584]{1,0:T(8,128)(2,1)} %param.6) | copy-start | bytes 1376260
  25.4 19.1 %copy-start.1 = (bf16[64,1]{0,1:T(2,128)(2,1)S(1)}, bf16[64,1]{0,1:T(2,128)(2,1)}, u32[]{:S(2)}) copy-start(bf16[64,1]{0,1:T(2,128)(2,1)} %param.8) | copy-start | bytes 388
  41.0 14.0 %all-to-all-start.1 = ((bf16[4,18,3584]{2,1,0:T(8,128)(2,1)}), bf16[4,18,3584]{2,1,0:T(8,128)(2,1)S(1)}, u32[]{:S(2)}, u32[]{:S(2)}) async-start(bf16[4,18,3584]{2,1,0:T(8,128)(2,1)} %reshape.61), calls=%async_computation.1 | async-start | bytes 1376256 | tf_op jit(solution)/shard_map/all_to_all | solution.py:39
where the time goes:
time: 56.7 us; the launch traced here: 56.4 us
  matrix products  24.1 us (43%)
  blocking collectives  14.6 us (26%)
  waiting for transfers between devices  10.5 us (19%)
  starting transfers between devices  3.48 us (6%)
  other arithmetic  2.38 us (4%)
  local copies, waits for them, and re-layouts  1.19 us (2%)
    all_to_all x1, blocking collectives, local(): lax.all_to_all(outgoing, 'expert', split_axis=0, concat_axis=0, tiled=True)  14.6 us
    dot_general x1, matrix products, local(): jnp.dot(hidden, w_down, preferred_element_type=jnp.float32)  14.6 us
    all_to_all x1, waiting for transfers between devices, local(): lax.all_to_all(result, 'expert', split_axis=0, concat_axis=0, tiled=True)  10.5 us
    dot_general x1, matrix products, local(): gate_values = jnp.dot(row_block, w_gate, preferred_element_type=jnp.float32)  7.85 us
    all_to_all x1, starting transfers between devices, local(): lax.all_to_all(result, 'expert', split_axis=0, concat_axis=0, tiled=True)  3.48 us
    dot_general x1, matrix products, local(): jnp.einsum('ecf,ecd->fd', weighted, summed, precision=lax.Precision.HIGHEST)  1.35 us
  transfers between devices with their start and end apart: 1, of which 1 were waited for; matrix products, arithmetic and copies ran while one was open for 0% of the time, Pallas kernels for 0%

commit v1 on v0

--- a/solution.py
+++ b/solution.py
@@ -6,6 +6,18 @@
 EXPERTS = 4
 TOP = 1
 CAP = 18
+
+
+def meet_record(u, dim_k, arr_in):
+    arr_out = u.shape
+    shaped = u.reshape(*arr_out[:dim_k], arr_in, arr_out[dim_k] // arr_in, *arr_out[dim_k + 1 :])
+    return jnp.moveaxis(shaped, dim_k, 0)
+
+
+def fill_yards(page, dim_no):
+    mid_arr = list(page.shape[1:])
+    mid_arr[dim_no] *= page.shape[0]
+    return jnp.moveaxis(page, 0, dim_no).reshape(mid_arr)
 
 
 def local(tokens, expert_ids, combine, w_gate, w_up, w_down):
@@ -25,7 +37,21 @@
         "ecf,fd->ecd", placed.astype(jnp.bfloat16), repeated, preferred_element_type=jnp.float32
     ).astype(jnp.bfloat16)
     outgoing = jnp.repeat(outgoing, span_size, axis=0)
-    arrived = lax.all_to_all(outgoing, "expert", split_axis=0, concat_axis=0, tiled=True)
+
+    def _return_all_panels(array_in, dev_axis, slab_in, local_block):
+        b_next = lax.axis_size(dev_axis)
+        z, wide_out = (b_next, lax.axis_index(dev_axis))
+        later = meet_record(array_in, slab_in, z)
+        frames = [later[wide_out]]
+        for rr in range(1, z):
+            moved = later[(wide_out + rr) % z]
+            frames.append(
+                lax.ppermute(moved, dev_axis, [(num, (num + rr) % z) for num in range(z)])
+            )
+        later = jnp.stack(frames)[(wide_out - jnp.arange(z)) % z]
+        return fill_yards(later, local_block)
+
+    arrived = _return_all_panels(outgoing, "expert", 0, 0)
     slot_count = arrived.shape[1]
     row_block = arrived.reshape(-1, model_width)
     gate_values = jnp.dot(row_block, w_gate, preferred_element_type=jnp.float32)

time: 56.7 us -> 53.9 us (0.951)
  blocking collectives: 14.6 us -> 0 us
  waiting for transfers between devices: 10.5 us -> 17.1 us
  starting transfers between devices: 3.48 us -> 7.99 us
  local copies, waits for them, and re-layouts: 1.19 us -> 1.87 us
    all_to_all x1 -> x0, blocking collectives: 14.6 us -> none  [local(): lax.all_to_all(outgoing, 'expert', split_axis=0, concat_axis=0, tiled=True)]
    ppermute x0 -> x3, waiting for transfers between devices: none -> 6.39 us  [_return_all_panels(): lax.ppermute(moved, dev_axis, [(num, (num + rr) % z) for num in range(z)])]
    ppermute x0 -> x3, starting transfers between devices: none -> 4.51 us  [_return_all_panels(): lax.ppermute(moved, dev_axis, [(num, (num + rr) % z) for num in range(z)])]
    gather x0 -> x1, local copies, waits for them, and re-layouts: none -> 0.59 us  [_return_all_panels(): later = jnp.stack(frames)[(wide_out - jnp.arange(z)) % z]]
  transfers between devices with their start and end apart: 1 -> 4, of which waited for: 1 -> 4; matrix products, arithmetic and copies ran while one was open for 0% -> 0% of each run, Pallas kernels for 0% -> 0%
where the time goes in v1:
time: 53.9 us; the launch traced here: 53.7 us
  matrix products  24.1 us (45%)
  waiting for transfers between devices  17.1 us (32%)
  starting transfers between devices  7.99 us (15%)
  other arithmetic  2.51 us (5%)
  local copies, waits for them, and re-layouts  1.87 us (3%)
    dot_general x1, matrix products, local(): jnp.dot(hidden, w_down, preferred_element_type=jnp.float32)  14.6 us
    all_to_all x1, waiting for transfers between devices, local(): lax.all_to_all(result, 'expert', split_axis=0, concat_axis=0, tiled=True)  10.7 us
    dot_general x1, matrix products, local(): gate_values = jnp.dot(row_block, w_gate, preferred_element_type=jnp.float32)  7.85 us
    ppermute x3, waiting for transfers between devices, _return_all_panels(): lax.ppermute(moved, dev_axis, [(num, (num + rr) % z) for num in range(z)])  6.39 us
    ppermute x3, starting transfers between devices, _return_all_panels(): lax.ppermute(moved, dev_axis, [(num, (num + rr) % z) for num in range(z)])  4.51 us
    all_to_all x1, starting transfers between devices, local(): lax.all_to_all(result, 'expert', split_axis=0, concat_axis=0, tiled=True)  3.48 us
    dot_general x1, matrix products, local(): jnp.einsum('ecf,ecd->fd', weighted, summed, precision=lax.Precision.HIGHEST)  1.35 us
  transfers between devices with their start and end apart: 4, of which 4 were waited for; matrix products, arithmetic and copies ran while one was open for 0% of the time, Pallas kernels for 0%

profile of v1, /device:TPU:0, one launch (start us, length us, event | category | flops | bytes accessed | tf_op | source)
XLA Modules:
  0.0 53.7 jit_solution(1783439300907811036)
XLA Ops:
  0.0 0.0 copy-start
  0.0 0.8 %fusion.5 = s32[64,4]{1,0:T(8,128)S(1)} fusion(s32[64]{0:T(128)} %bitcast.29), kind=kLoop, calls=%fused_computation.15 | loop fusion | flops 512 | bytes 1280 | tf_op jit(solution)/shard_map/convert_element_type | solution.py:30
  0.8 0.7 %convert_compare_fusion = pred[4,64]{1,0:T(4,128)(4,1)S(1)} fusion(s32[64]{0:T(128)} %bitcast.30), kind=kLoop, calls=%fused_computation.27 | loop fusion | flops 768 | bytes 512 | tf_op jit(solution)/shard_map/eq | solution.py:34
  1.4 0.1 reduce_window_sum.11
  1.5 0.8 %select_reduce_fusion = s32[64]{0:T(128)S(1)} fusion(s32[64,4]{1,0:T(8,128)S(1)} %reduce_window_sum.11, s32[64]{0:T(128)} %bitcast.31), kind=kLoop, calls=%fused_computation.13 | loop fusion | flops 960 | bytes 1536 | tf_op jit(solution)/shard_map/reduce_sum | solution.py:32
  2.4 0.0 copy-done
  2.4 0.3 convolution_convert_fusion
  2.7 0.1 dynamic-slice_bitcast_fusion
  2.8 0.5 %collective-permute-start = (bf16[1,18,3584]{2,1,0:T(8,128)(2,1)S(1)}, bf16[1,18,3584]{2,1,0:T(8,128)(2,1)S(1)}, u32[]{:S(2)}, u32[]{:S(2)}) collective-permute-start(bf16[1,18,3584]{2,1,0:T(8,128)(2,1)S(1)} %get-tuple-element.8), channel_id=1, source_target_pairs={{0,8},{8,16},{16,24},{24,0},{1,9},{9,17},{17,25},{25,1},{2,10},{10... | collective-permute-start | bytes 387080 | tf_op jit(solution)/shard_map/ppermute | solution.py:49
  3.4 2.6 %collective-permute-start.1 = (bf16[1,18,3584]{2,1,0:T(8,128)(2,1)S(1)}, bf16[1,18,3584]{2,1,0:T(8,128)(2,1)S(1)}, u32[]{:S(2)}, u32[]{:S(2)}) collective-permute-start(bf16[1,18,3584]{2,1,0:T(8,128)(2,1)S(1)} %get-tuple-element.7), channel_id=1, source_target_pairs={{0,16},{8,24},{16,0},{24,8},{1,17},{9,25},{17,1},{25,9},{2,18},{10... | collective-permute-start | bytes 387080 | tf_op jit(solution)/shard_map/ppermute | solution.py:49
  5.9 1.4 %collective-permute-start.2 = (bf16[1,18,3584]{2,1,0:T(8,128)(2,1)S(1)}, bf16[1,18,3584]{2,1,0:T(8,128)(2,1)S(1)}, u32[]{:S(2)}, u32[]{:S(2)}) collective-permute-start(bf16[1,18,3584]{2,1,0:T(8,128)(2,1)S(1)} %get-tuple-element.6), channel_id=1, source_target_pairs={{0,24},{8,0},{16,8},{24,16},{1,25},{9,1},{17,9},{25,17},{2,26},{10... | collective-permute-start | bytes 387080 | tf_op jit(solution)/shard_map/ppermute | solution.py:49
  7.4 1.9 %collective-permute-done = bf16[1,18,3584]{2,1,0:T(8,128)(2,1)S(1)} collective-permute-done((bf16[1,18,3584]{2,1,0:T(8,128)(2,1)S(1)}, bf16[1,18,3584]{2,1,0:T(8,128)(2,1)S(1)}, u32[]{:S(2)}, u32[]{:S(2)}) %collective-permute-start) | collective-permute-done | bytes 129056 | tf_op jit(solution)/shard_map/ppermute | solution.py:49
  9.3 1.9 %collective-permute-done.1 = bf16[1,18,3584]{2,1,0:T(8,128)(2,1)S(1)} collective-permute-done((bf16[1,18,3584]{2,1,0:T(8,128)(2,1)S(1)}, bf16[1,18,3584]{2,1,0:T(8,128)(2,1)S(1)}, u32[]{:S(2)}, u32[]{:S(2)}) %collective-permute-start.1) | collective-permute-done | bytes 129056 | tf_op jit(solution)/shard_map/ppermute | solution.py:49
  11.2 2.6 %collective-permute-done.2 = bf16[1,18,3584]{2,1,0:T(8,128)(2,1)S(1)} collective-permute-done((bf16[1,18,3584]{2,1,0:T(8,128)(2,1)S(1)}, bf16[1,18,3584]{2,1,0:T(8,128)(2,1)S(1)}, u32[]{:S(2)}, u32[]{:S(2)}) %collective-permute-start.2) | collective-permute-done | bytes 129056 | tf_op jit(solution)/shard_map/ppermute | solution.py:49
  13.7 0.1 maximum_bitcast_fusion
  13.9 0.6 %gather_fusion = bf16[4,18,3584]{2,1,0:T(8,128)(2,1)S(1)} fusion(bf16[4,18,3584]{2,1,0:T(8,128)(2,1)S(1)} %maximum_bitcast_fusion, s32[1024]{0:T(1024)S(1)} %pad_clamp_fusion), kind=kCustom, calls=%fused_computation | custom fusion | bytes 1032208 | tf_op jit(solution)/shard_map/gather | solution.py:51
  14.5 0.2 reshape_reshape.3
  14.6 7.8 %fusion.16 = f32[72,2048]{1,0:T(8,128)S(1)} fusion(bf16[72,3584]{1,0:T(8,128)(2,1)S(1)} %reshape_reshape.3, bf16[3584,2048]{1,0:T(8,128)(2,1)} %param.9), kind=kOutput, calls=%fused_computation.38 | convolution fusion | flops 1056964608 | bytes 15785984 | tf_op jit(solution)/shard_map/dot_general | solution.py:57
  22.5 0.0 copy-start.1
  22.5 14.6 %convolution_convert_fusion.1 = bf16[72,3584]{1,0:T(8,128)(2,1)S(1)} fusion(bf16[2048,3584]{1,0:T(8,128)(2,1)} %param.11, bf16[72,3584]{1,0:T(8,128)(2,1)S(1)} %reshape_reshape.3, bf16[3584,2048]{1,0:T(8,128)(2,1)} %param.10, f32[72,2048]{1,0:T(8,128)S(1)} %fusion.16), kind=kOutput, calls=%fused_computation.3 | convolution fusion | flops 2115072000 | bytes 30982144 | tf_op jit(solution)/shard_map/dot_general | solution.py:61
  37.1 1.0 %reshape.113 = bf16[4,18,3584]{2,1,0:T(8,128)(2,1)} reshape(bf16[72,3584]{1,0:T(8,128)(2,1)S(1)} %convolution_convert_fusion.1) | data formatting | bytes 1032192 | tf_op jit(solution)/shard_map/reshape | solution.py:63
  38.1 3.5 %all-to-all-start = ((bf16[4,18,3584]{2,1,0:T(8,128)(2,1)}), bf16[4,18,3584]{2,1,0:T(8,128)(2,1)S(1)}, u32[]{:S(2)}, u32[]{:S(2)}) async-start(bf16[4,18,3584]{2,1,0:T(8,128)(2,1)} %reshape.113), calls=%async_computation | async-start | bytes 1376256 | tf_op jit(solution)/shard_map/all_to_all | solution.py:65
  41.6 0.0 copy-done.1
  41.6 10.7 %all-to-all-done = bf16[4,18,3584]{2,1,0:T(8,128)(2,1)S(1)} async-done(((bf16[4,18,3584]{2,1,0:T(8,128)(2,1)}), bf16[4,18,3584]{2,1,0:T(8,128)(2,1)S(1)}, u32[]{:S(2)}, u32[]{:S(2)}) %all-to-all-start) | async-done | bytes 516128 | tf_op jit(solution)/shard_map/all_to_all | solution.py:65
  52.3 1.4 %fusion = bf16[64,3584]{1,0:T(8,128)(2,1)} fusion(bf16[4,18,3584]{2,1,0:T(8,128)(2,1)S(1)} %all-to-all-done, f32[64]{0:T(128)S(1)} %bitcast_convert_fusion, pred[18,64]{1,0:T(8,128)(4,1)S(1)} %iota_compare_fusion.1, pred[4,64]{1,0:T(4,128)(4,1)S(1)} %convert_compare_fusion), kind=kOutput, calls=%fused_computation.4 | convolution fusion | flops 198419456 | bytes 976512 | tf_op jit(solution)/shard_map/ecf,ecd->fd/dot_general | solution.py:70
  (4 shorter events, 0.0 us)
Async XLA Ops:
  0.0 2.4 %copy-start = (bf16[64,3584]{1,0:T(8,128)(2,1)S(1)}, bf16[64,3584]{1,0:T(8,128)(2,1)}, u32[]{:S(2)}) copy-start(bf16[64,3584]{1,0:T(8,128)(2,1)} %param.6) | copy-start | bytes 1376260
  2.8 6.5 %collective-permute-start = (bf16[1,18,3584]{2,1,0:T(8,128)(2,1)S(1)}, bf16[1,18,3584]{2,1,0:T(8,128)(2,1)S(1)}, u32[]{:S(2)}, u32[]{:S(2)}) collective-permute-start(bf16[1,18,3584]{2,1,0:T(8,128)(2,1)S(1)} %get-tuple-element.8), channel_id=1, source_target_pairs={{0,8},{8,16},{16,24},{24,0},{1,9},{9,17},{17,25},{25,1},{2,10},{10... | collective-permute-start | bytes 387080 | tf_op jit(solution)/shard_map/ppermute | solution.py:49
  3.4 7.8 %collective-permute-start.1 = (bf16[1,18,3584]{2,1,0:T(8,128)(2,1)S(1)}, bf16[1,18,3584]{2,1,0:T(8,128)(2,1)S(1)}, u32[]{:S(2)}, u32[]{:S(2)}) collective-permute-start(bf16[1,18,3584]{2,1,0:T(8,128)(2,1)S(1)} %get-tuple-element.7), channel_id=1, source_target_pairs={{0,16},{8,24},{16,0},{24,8},{1,17},{9,25},{17,1},{25,9},{2,18},{10... | collective-permute-start | bytes 387080 | tf_op jit(solution)/shard_map/ppermute | solution.py:49
  5.9 7.8 %collective-permute-start.2 = (bf16[1,18,3584]{2,1,0:T(8,128)(2,1)S(1)}, bf16[1,18,3584]{2,1,0:T(8,128)(2,1)S(1)}, u32[]{:S(2)}, u32[]{:S(2)}) collective-permute-start(bf16[1,18,3584]{2,1,0:T(8,128)(2,1)S(1)} %get-tuple-element.6), channel_id=1, source_target_pairs={{0,24},{8,0},{16,8},{24,16},{1,25},{9,1},{17,9},{25,17},{2,26},{10... | collective-permute-start | bytes 387080 | tf_op jit(solution)/shard_map/ppermute | solution.py:49
  22.5 19.1 %copy-start.1 = (bf16[64,1]{0,1:T(2,128)(2,1)S(1)}, bf16[64,1]{0,1:T(2,128)(2,1)}, u32[]{:S(2)}) copy-start(bf16[64,1]{0,1:T(2,128)(2,1)} %param.8) | copy-start | bytes 388
  38.1 14.2 %all-to-all-start = ((bf16[4,18,3584]{2,1,0:T(8,128)(2,1)}), bf16[4,18,3584]{2,1,0:T(8,128)(2,1)S(1)}, u32[]{:S(2)}, u32[]{:S(2)}) async-start(bf16[4,18,3584]{2,1,0:T(8,128)(2,1)} %reshape.113), calls=%async_computation | async-start | bytes 1376256 | tf_op jit(solution)/shard_map/all_to_all | solution.py:65
